TPU v7x, 32 devices: a whole 2x2x4 slice. The times are simulated.
32 devices in a mesh: rows: 8 (over y, x, core), cols: 4 (over z).
Axes of the slice: x: 2, y: 2, z: 4, core: 2. Of those that a mesh axis runs over, the one named last changes fastest.
Arguments:
- coords: int32 [8, 16384], P(None, ('rows', 'cols')), may hold values from 0 to 4095
- probes: float32 [64, 16384], P(None, ('rows', 'cols')), may hold values from -6 to 6
- lengthscales: float32 [8], replicated, may hold values from 0.15 to 0.25
- amplitude: float32 [1], replicated, may hold values from 0.1 to 0.3
- landmarks: float32 [14, 8, 128], replicated, may hold values from 0 to 1
- coupling: float32 [128, 128], replicated, may hold values from -0.5 to 0.5
Outputs:
- products: float32 [2, 64, 16384], P(None, None, ('rows', 'cols'))
All inputs are finite; a program needn't handle non-finite values.
Results may differ from a plain program's by a relative error of at most 0.0025.
Values may be sent and summed in bfloat16 or wider, within the bound.
A program may use at most 64 MiB of HBM per device.

v0:
```python
import jax
import jax.numpy as jnp
from jax import lax
from jax.sharding import PartitionSpec as P


def swapped(array, axis, apart):
    return lax.ppermute(array, axis, [(i, i ^ 1 << apart) for i in range(lax.axis_size(axis))])


def pair_squares(left_points, right_points):
    squared = jnp.zeros((left_points.shape[1], right_points.shape[1]), jnp.float32)
    for component in range(left_points.shape[0]):
        offset = left_points[component][:, None] - right_points[component][None, :]
        squared = squared + offset * offset
    return squared


def on_device(coords, probes, lengthscales, amplitude, landmarks, coupling):
    highest = lax.Precision.HIGHEST
    inverse_scale = 1.0 / lengthscales
    scaled = coords.astype(jnp.float32) * (1.0 / 4096.0) * inverse_scale[:, None]
    strength = amplitude[0]
    signs_half = probes.astype(jnp.bfloat16)
    width = coords.shape[1]
    groups = lax.axis_size("cols")
    rows_index = lax.axis_index("rows")
    levels = lax.axis_size("rows").bit_length() - 1
    leaf_points = lax.all_gather(scaled, "cols", axis=1, tiled=True)
    leaf_signs = lax.all_gather(signs_half, "cols", axis=1, tiled=True)
    accumulated = jnp.zeros((2, probes.shape[0], width), jnp.float32)
    for row_block in range(groups):
        block_points = leaf_points[:, row_block * width : (row_block + 1) * width]
        block_signs = leaf_signs[:, row_block * width : (row_block + 1) * width]
        squared = pair_squares(block_points, scaled)
        kernel = strength * jnp.exp(-0.5 * squared)
        kernel_half = kernel.astype(jnp.bfloat16)
        slope_half = (kernel * squared).astype(jnp.bfloat16)
        accumulated = accumulated + jnp.stack(
            [
                jnp.dot(block_signs, kernel_half, preferred_element_type=jnp.float32),
                jnp.dot(block_signs, slope_half, preferred_element_type=jnp.float32),
            ]
        )
    result = accumulated
    factor_list = []
    dfactor_list = []
    for level in range(levels):
        depth = levels - level
        node = jnp.right_shift(rows_index, level)
        chosen = lax.dynamic_index_in_dim(landmarks, 2**depth - 2 + node, 0, keepdims=False)
        squared = pair_squares(scaled, chosen * inverse_scale[:, None])
        factor = strength * jnp.exp(-0.5 * squared)
        factor_list.append(factor)
        dfactor_list.append(factor * squared)
    factor_stack = jnp.stack(factor_list)
    dfactor_stack = jnp.stack(dfactor_list)
    own_project = jnp.einsum("pn,lnr->lpr", probes, factor_stack, precision=highest)
    own_dproject = jnp.einsum("pn,lnr->lpr", probes, dfactor_stack, precision=highest)
    projections = lax.psum(jnp.stack([own_project, own_dproject], axis=1), "cols")
    siblings = []
    pending = projections
    for level in range(levels):
        partner = swapped(pending[level:], "rows", level)
        siblings.append(partner[0])
        pending = pending.at[level + 1 :].add(partner[1:])
    for level in range(levels):
        sibling_sums = siblings[level]
        is_left = jnp.right_shift(rows_index, level) & 1 == 0
        core = jnp.where(is_left, coupling.T, coupling)
        first = jnp.dot(sibling_sums[0], core, precision=highest)
        second = jnp.dot(sibling_sums[1], core, precision=highest)
        value = jnp.dot(first, factor_stack[level].T, precision=highest)
        slope = jnp.dot(first, dfactor_stack[level].T, precision=highest) + jnp.dot(
            second, factor_stack[level].T, precision=highest
        )
        result = result + jnp.stack([value, slope])
    return result


def solution(mesh):
    in_specs = (P(None, ("rows", "cols")), P(None, ("rows", "cols")), P(), P(), P(), P())
    out_specs = P(None, None, ("rows", "cols"))
    return jax.shard_map(
        on_device, mesh=mesh, in_specs=in_specs, out_specs=out_specs, check_vma=False
    )
```

profile of v0, /device:TPU:0, one launch (start us, length us, event | category | flops | bytes accessed | tf_op | source)
XLA Modules:
  0.0 75.2 jit_solution(17061877505005976449)
XLA Ops:
  6.5 0.7 copy-done.4
  7.2 0.0 copy-done.3
  7.3 0.1 convert_multiply_fusion
  8.0 0.8 %bitcast_multiply_fusion.2 = (f32[8,128]{1,0:T(8,128)S(1)}, f32[8,128]{1,0:T(8,128)S(1)}, f32[8,128]{1,0:T(8,128)S(1)}) fusion(f32[14,8,128]{2,1,0:T(8,128)} %param.14, s32[]{:T(128)S(6)} %select_n.30, f32[8]{0:T(128)S(1)} %get-tuple-element.30, s32[]{:T(128)S(6)} %select_n.32, s32[]{:T(128)S(6)} %select_n.31), kind=kLoop, calls=%fused_computation.137 | loop fusion | flops 3072 | bytes 24620 | tf_op jit(solution)/shard_map/mul | solution.py:52
  8.8 0.6 exponential_multiply_fusion.17
  9.4 0.6 exponential_multiply_fusion.16
  10.1 0.0 copy-start.1
  10.1 0.6 exponential_multiply_fusion.18
  10.7 0.3 copy-done.1
  11.0 0.6 convolution_bitcast_fusion.12
  11.6 0.6 convolution_bitcast_fusion.11
  12.1 0.7 pad_maximum_fusion
  12.8 0.0 all-reduce.2.cloned.1.call-update
  12.9 15.0 %all_gather.6 = f32[8,2048]{1,0:T(8,128)S(1)} all-gather(f32[8,512]{1,0:T(8,128)S(1)} %convert_multiply_fusion), channel_id=1, replica_groups=mesh['rows'=8,'cols'=4] {'cols'}, dimensions={1}, use_global_device_ids=true | all-gather | bytes 81920 | tf_op jit(solution)/shard_map/all_gather | solution.py:29
  27.9 0.0 copy-start
  28.0 0.8 %copy-done = f32[128,128]{1,0:T(8,128)S(1)} copy-done((f32[128,128]{1,0:T(8,128)S(1)}, f32[128,128]{1,0:T(8,128)}, u32[]{:S(2)}) %copy-start) | copy-done | bytes 65560
  28.8 0.1 copy.7
  28.9 14.7 %all_gather.7 = bf16[64,2048]{1,0:T(8,128)(2,1)S(1)} all-gather(bf16[64,512]{1,0:T(8,128)(2,1)S(1)} %convert_element_type.32), channel_id=1, replica_groups=mesh['rows'=8,'cols'=4] {'cols'}, dimensions={1}, use_global_device_ids=true | all-gather | bytes 327680 | tf_op jit(solution)/shard_map/all_gather | solution.py:30
  43.5 1.1 %convolution_bitcast_fusion.1 = f32[1,64,512]{2,1,0:T(8,128)S(1)} fusion(f32[]{:T(128)} %bitcast.196, f32[512]{0:T(512)S(1)} %bitcast.393, f32[512]{0:T(512)S(1)} %bitcast.395, f32[512]{0:T(512)S(1)} %bitcast.397, f32[512]{0:T(512)S(1)} %bitcast.399, f32[512]{0:T(512)S(1)} %bitcast.401, f32[512]{0:T(512)S(1)} %bitcast.403, f32[512]{0:T(512)S(1)} %bitcast.405, ...), kind=kOutput, calls=%fused_computation.1 | convolution fusion | flops 40370176 | bytes 229380 | tf_op jit(solution)/shard_map/dot_general | solution.py:41
  44.7 1.2 %convolution_bitcast_fusion = f32[1,64,512]{2,1,0:T(8,128)S(1)} fusion(f32[]{:T(128)} %bitcast.195, f32[512]{0:T(512)S(1)} %bitcast.394, f32[512]{0:T(512)S(1)} %bitcast.396, f32[512]{0:T(512)S(1)} %bitcast.398, f32[512]{0:T(512)S(1)} %bitcast.400, f32[512]{0:T(512)S(1)} %bitcast.402, f32[512]{0:T(512)S(1)} %bitcast.404, f32[512]{0:T(512)S(1)} %bitcast.406, ...), kind=kOutput, calls=%fused_computation | convolution fusion | flops 40632320 | bytes 229380 | tf_op jit(solution)/shard_map/dot_general | solution.py:42
  45.9 1.1 %convolution_bitcast_fusion.3 = f32[1,64,512]{2,1,0:T(8,128)S(1)} fusion(f32[]{:T(128)} %bitcast.197, f32[512]{0:T(512)S(1)} %bitcast.375, f32[512]{0:T(512)S(1)} %bitcast.377, f32[512]{0:T(512)S(1)} %bitcast.379, f32[512]{0:T(512)S(1)} %bitcast.381, f32[512]{0:T(512)S(1)} %bitcast.383, f32[512]{0:T(512)S(1)} %bitcast.385, f32[512]{0:T(512)S(1)} %bitcast.387, ...), kind=kOutput, calls=%fused_computation.3 | convolution fusion | flops 40370176 | bytes 229380 | tf_op jit(solution)/shard_map/dot_general | solution.py:41
  47.1 1.2 %convolution_bitcast_fusion.2 = f32[1,64,512]{2,1,0:T(8,128)S(1)} fusion(f32[]{:T(128)} %bitcast.194, f32[512]{0:T(512)S(1)} %bitcast.376, f32[512]{0:T(512)S(1)} %bitcast.378, f32[512]{0:T(512)S(1)} %bitcast.380, f32[512]{0:T(512)S(1)} %bitcast.382, f32[512]{0:T(512)S(1)} %bitcast.384, f32[512]{0:T(512)S(1)} %bitcast.386, f32[512]{0:T(512)S(1)} %bitcast.388, ...), kind=kOutput, calls=%fused_computation.2 | convolution fusion | flops 40632320 | bytes 229380 | tf_op jit(solution)/shard_map/dot_general | solution.py:42
  48.3 1.1 %convolution_bitcast_fusion.5 = f32[1,64,512]{2,1,0:T(8,128)S(1)} fusion(f32[]{:T(128)} %bitcast.198, f32[512]{0:T(512)S(1)} %bitcast.369, f32[512]{0:T(512)S(1)} %bitcast.371, f32[512]{0:T(512)S(1)} %bitcast.373, f32[512]{0:T(512)S(1)} %bitcast.425, f32[512]{0:T(512)S(1)} %bitcast.427, f32[512]{0:T(512)S(1)} %bitcast.429, f32[512]{0:T(512)S(1)} %bitcast.431, ...), kind=kOutput, calls=%fused_computation.5 | convolution fusion | flops 40370176 | bytes 229380 | tf_op jit(solution)/shard_map/dot_general | solution.py:41
  49.4 1.2 %convolution_bitcast_fusion.4 = f32[1,64,512]{2,1,0:T(8,128)S(1)} fusion(f32[]{:T(128)} %bitcast.193, f32[512]{0:T(512)S(1)} %bitcast.370, f32[512]{0:T(512)S(1)} %bitcast.372, f32[512]{0:T(512)S(1)} %bitcast.374, f32[512]{0:T(512)S(1)} %bitcast.426, f32[512]{0:T(512)S(1)} %bitcast.428, f32[512]{0:T(512)S(1)} %bitcast.430, f32[512]{0:T(512)S(1)} %bitcast.432, ...), kind=kOutput, calls=%fused_computation.4 | convolution fusion | flops 40632320 | bytes 229380 | tf_op jit(solution)/shard_map/dot_general | solution.py:42
  50.6 1.1 %convolution_bitcast_fusion.7 = f32[1,64,512]{2,1,0:T(8,128)S(1)} fusion(f32[]{:T(128)} %bitcast.189, f32[512]{0:T(512)S(1)} %bitcast.238, f32[512]{0:T(512)S(1)} %bitcast.407, f32[512]{0:T(512)S(1)} %bitcast.258, f32[512]{0:T(512)S(1)} %bitcast.409, f32[512]{0:T(512)S(1)} %bitcast.278, f32[512]{0:T(512)S(1)} %bitcast.411, f32[512]{0:T(512)S(1)} %bitcast.298, ...), kind=kOutput, calls=%fused_computation.7 | convolution fusion | flops 40370176 | bytes 229380 | tf_op jit(solution)/shard_map/dot_general | solution.py:41
  51.8 0.0 all-reduce.2.cloned.1.call-done
  51.8 0.1 collective-permute-start
  51.9 1.2 %convolution_bitcast_fusion.6 = f32[1,64,512]{2,1,0:T(8,128)S(1)} fusion(f32[]{:T(128)} %bitcast.192, f32[512]{0:T(512)S(1)} %bitcast.239, f32[512]{0:T(512)S(1)} %bitcast.408, f32[512]{0:T(512)S(1)} %bitcast.259, f32[512]{0:T(512)S(1)} %bitcast.410, f32[512]{0:T(512)S(1)} %bitcast.279, f32[512]{0:T(512)S(1)} %bitcast.412, f32[512]{0:T(512)S(1)} %bitcast.299, ...), kind=kOutput, calls=%fused_computation.6 | convolution fusion | flops 40632320 | bytes 229380 | tf_op jit(solution)/shard_map/dot_general | solution.py:42
  53.1 0.4 collective-permute-done
  53.6 1.3 %collective-permute-start.1 = (f32[2,2,64,128]{3,2,0,1:T(8,128)S(1)}, f32[2,2,64,128]{3,2,0,1:T(8,128)S(1)}, u32[]{:S(2)}, u32[]{:S(2)}) collective-permute-start(f32[2,2,64,128]{3,2,0,1:T(8,128)S(1)} %slice_add_fusion), channel_id=1, source_target_pairs={{0,8},{4,12},{8,0},{12,4},{16,24},{20,28},{24,16},{28,20},{1,9},{5... | collective-permute-start | bytes 393224 | tf_op jit(solution)/shard_map/ppermute | solution.py:8
  54.9 0.2 fusion.84
  55.1 1.0 %fusion.46 = f32[64,512]{1,0:T(8,128)S(1)} fusion(f32[64,128]{1,0:T(8,128)S(1)} %fusion.84, f32[]{:T(128)} %bitcast.199, f32[128]{0:T(128)S(1)} %get-tuple-element.81, f32[512]{0:T(512)S(1)} %bitcast.240, f32[128]{0:T(128)S(1)} %get-tuple-element.82, f32[512]{0:T(512)S(1)} %bitcast.260, f32[128]{0:T(128)S(1)} %get-tuple-element.83, f32[512]{0:T(512)S(1)} %bitcast.280, ...), kind=kOutput, calls=%fused_computation.75 | convolution fusion | flops 52035584 | bytes 184324 | tf_op jit(solution)/shard_map/dot_general | solution.py:74
  56.1 0.2 fusion.83
  56.3 1.0 %fusion.2 = f32[1,64,512]{2,1,0:T(8,128)S(1)} fusion(f32[64,512]{1,0:T(8,128)S(1)} %fusion.46, f32[64,128]{1,0:T(8,128)S(1)} %fusion.83, f32[]{:T(128)} %bitcast.200, f32[128]{0:T(128)S(1)} %get-tuple-element.81, f32[512]{0:T(512)S(1)} %bitcast.241, f32[128]{0:T(128)S(1)} %get-tuple-element.82, f32[512]{0:T(512)S(1)} %bitcast.261, ...), kind=kOutput, calls=%fused_computation.16 | convolution fusion | flops 52002816 | bytes 315396 | tf_op jit(solution)/shard_map/dot_general | solution.py:74
  57.3 1.0 %convolution_bitcast_fusion.10 = f32[1,64,512]{2,1,0:T(8,128)S(1)} fusion(f32[64,128]{1,0:T(8,128)S(1)} %fusion.84, f32[]{:T(128)} %bitcast.191, f32[128]{0:T(128)S(1)} %get-tuple-element.81, f32[512]{0:T(512)S(1)} %bitcast.242, f32[128]{0:T(128)S(1)} %get-tuple-element.82, f32[512]{0:T(512)S(1)} %bitcast.262, f32[128]{0:T(128)S(1)} %get-tuple-element.83, ...), kind=kOutput, calls=%fused_computation.10 | convolution fusion | flops 51970048 | bytes 184324 | tf_op jit(solution)/shard_map/dot_general | solution.py:73
  58.2 0.9 %collective-permute-done.1 = f32[2,2,64,128]{3,2,0,1:T(8,128)S(1)} collective-permute-done((f32[2,2,64,128]{3,2,0,1:T(8,128)S(1)}, f32[2,2,64,128]{3,2,0,1:T(8,128)S(1)}, u32[]{:S(2)}, u32[]{:S(2)}) %collective-permute-start.1) | collective-permute-done | bytes 131104 | tf_op jit(solution)/shard_map/ppermute | solution.py:8
  59.2 1.4 %collective-permute-start.2 = (f32[1,2,64,128]{3,2,0,1:T(8,128)S(1)}, f32[1,2,64,128]{3,2,0,1:T(8,128)S(1)}, u32[]{:S(2)}, u32[]{:S(2)}) collective-permute-start(f32[1,2,64,128]{3,2,0,1:T(8,128)S(1)} %slice_add_fusion.1), channel_id=1, source_target_pairs={{0,16},{4,20},{8,24},{12,28},{16,0},{20,4},{24,8},{28,12},{1,17},{... | collective-permute-start | bytes 196616 | tf_op jit(solution)/shard_map/ppermute | solution.py:8
  60.6 0.2 fusion.82
  60.7 1.2 %fusion.44 = f32[64,512]{1,0:T(8,128)S(1)} fusion(f32[64,128]{1,0:T(8,128)S(1)} %fusion.82, f32[]{:T(128)} %bitcast.201, f32[128]{0:T(128)S(1)} %get-tuple-element.110, f32[128]{0:T(128)S(1)} %get-tuple-element.109, f32[128]{0:T(128)S(1)} %get-tuple-element.108, f32[128]{0:T(128)S(1)} %get-tuple-element.107, f32[128]{0:T(128)S(1)} %get-tuple-element.106, ...), kind=kOutput, calls=%fused_computation.71 | convolution fusion | flops 52035584 | bytes 184324 | tf_op jit(solution)/shard_map/dot_general | solution.py:74
  62.0 0.2 fusion.81
  62.1 1.0 %fusion.1 = f32[1,64,512]{2,1,0:T(8,128)S(1)} fusion(f32[64,512]{1,0:T(8,128)S(1)} %fusion.44, f32[64,128]{1,0:T(8,128)S(1)} %fusion.81, f32[]{:T(128)} %bitcast.202, f32[128]{0:T(128)S(1)} %get-tuple-element.110, f32[128]{0:T(128)S(1)} %get-tuple-element.109, f32[128]{0:T(128)S(1)} %get-tuple-element.108, f32[128]{0:T(128)S(1)} %get-tuple-element.107, ...), kind=kOutput, calls=%fused_computation.14 | convolution fusion | flops 52002816 | bytes 315396 | tf_op jit(solution)/shard_map/dot_general | solution.py:74
  63.1 1.0 %convolution_bitcast_fusion.9 = f32[1,64,512]{2,1,0:T(8,128)S(1)} fusion(f32[64,128]{1,0:T(8,128)S(1)} %fusion.82, f32[]{:T(128)} %bitcast.206, f32[128]{0:T(128)S(1)} %get-tuple-element.110, f32[128]{0:T(128)S(1)} %get-tuple-element.109, f32[128]{0:T(128)S(1)} %get-tuple-element.108, f32[128]{0:T(128)S(1)} %get-tuple-element.107, ...), kind=kOutput, calls=%fused_computation.9 | convolution fusion | flops 51970048 | bytes 184324 | tf_op jit(solution)/shard_map/dot_general | solution.py:73
  64.1 0.2 fusion.80
  64.3 1.0 %convolution_bitcast_fusion.8 = f32[1,64,512]{2,1,0:T(8,128)S(1)} fusion(f32[64,128]{1,0:T(8,128)S(1)} %fusion.80, f32[]{:T(128)} %bitcast.205, f32[128]{0:T(128)S(1)} %get-tuple-element.97, f32[128]{0:T(128)S(1)} %get-tuple-element.98, f32[128]{0:T(128)S(1)} %get-tuple-element.99, f32[128]{0:T(128)S(1)} %get-tuple-element.100, ...), kind=kOutput, calls=%fused_computation.8 | convolution fusion | flops 51970048 | bytes 184324 | tf_op jit(solution)/shard_map/dot_general | solution.py:73
  65.3 1.0 %fusion.42 = f32[64,512]{1,0:T(8,128)S(1)} fusion(f32[64,128]{1,0:T(8,128)S(1)} %fusion.80, f32[]{:T(128)} %bitcast.203, f32[128]{0:T(128)S(1)} %get-tuple-element.97, f32[128]{0:T(128)S(1)} %get-tuple-element.98, f32[128]{0:T(128)S(1)} %get-tuple-element.99, f32[128]{0:T(128)S(1)} %get-tuple-element.100, f32[128]{0:T(128)S(1)} %get-tuple-element.101, ...), kind=kOutput, calls=%fused_computation.67 | convolution fusion | flops 52035584 | bytes 184324 | tf_op jit(solution)/shard_map/dot_general | solution.py:74
  66.3 0.2 fusion.79
  66.5 1.0 %fusion = f32[1,64,512]{2,1,0:T(8,128)S(1)} fusion(f32[64,512]{1,0:T(8,128)S(1)} %fusion.42, f32[64,128]{1,0:T(8,128)S(1)} %fusion.79, f32[]{:T(128)} %bitcast.204, f32[128]{0:T(128)S(1)} %get-tuple-element.97, f32[128]{0:T(128)S(1)} %get-tuple-element.98, f32[128]{0:T(128)S(1)} %get-tuple-element.99, f32[128]{0:T(128)S(1)} %get-tuple-element.100, ...), kind=kOutput, calls=%fused_computation.12 | convolution fusion | flops 52002816 | bytes 315396 | tf_op jit(solution)/shard_map/dot_general | solution.py:74
  67.5 0.9 %fusion.41 = f32[2,64,512]{2,1,0:T(8,128)} fusion(f32[1,64,512]{2,1,0:T(8,128)S(1)} %convolution_bitcast_fusion.6, f32[1,64,512]{2,1,0:T(8,128)S(1)} %convolution_bitcast_fusion.7, f32[1,64,512]{2,1,0:T(8,128)S(1)} %convolution_bitcast_fusion.4, f32[1,64,512]{2,1,0:T(8,128)S(1)} %convolution_bitcast_fusion.5, ...), kind=kLoop, calls=%fused_computation.66 | loop fusion | flops 851968 | bytes 2097152 | tf_op jit(solution)/shard_map/add | solution.py:77
  (15 shorter events, 0.1 us)
Async XLA Ops:
  6.5 0.7 copy-start.3
  6.5 45.3 %all-reduce.2.cloned.1.call-start = ((), (), s32[]{:S(2)}) async-start(), calls=%async_computation | async-start | bytes 393216 | tf_op jit(solution)/shard_map/psum | solution.py:60
  6.5 0.7 copy-start.4
  10.1 0.9 %copy-start.1 = (f32[64,512]{1,0:T(8,128)S(1)}, f32[64,512]{1,0:T(8,128)}, u32[]{:S(2)}) copy-start(f32[64,512]{1,0:T(8,128)} %param.11) | copy-start | bytes 393220
  27.9 0.8 %copy-start = (f32[128,128]{1,0:T(8,128)S(1)}, f32[128,128]{1,0:T(8,128)}, u32[]{:S(2)}) copy-start(f32[128,128]{1,0:T(8,128)} %param.15) | copy-start | bytes 196612
  51.8 1.7 %collective-permute-start = (f32[3,2,64,128]{3,2,0,1:T(8,128)}, f32[3,2,64,128]{3,2,0,1:T(8,128)S(1)}, u32[]{:S(2)}, u32[]{:S(2)}) collective-permute-start(f32[3,2,64,128]{3,2,0,1:T(8,128)} %all-reduce.2.cloned.1.call-done), channel_id=1, source_target_pairs={{0,4},{4,0},{8,12},{12,8},{16,20},{20,16},{24,28},{28,24},{1,5},{5... | collective-permute-start | bytes 589832 | tf_op jit(solution)/shard_map/ppermute | solution.py:8
  51.9 1.6 %copy-start.2 = (f32[3,2,64,128]{3,2,0,1:T(8,128)S(1)}, f32[3,2,64,128]{3,2,0,1:T(8,128)}, u32[]{:S(2)}) copy-start(f32[3,2,64,128]{3,2,0,1:T(8,128)} %all-reduce.2.cloned.1.call-done) | copy-start | bytes 589828
  53.6 5.6 %collective-permute-start.1 = (f32[2,2,64,128]{3,2,0,1:T(8,128)S(1)}, f32[2,2,64,128]{3,2,0,1:T(8,128)S(1)}, u32[]{:S(2)}, u32[]{:S(2)}) collective-permute-start(f32[2,2,64,128]{3,2,0,1:T(8,128)S(1)} %slice_add_fusion), channel_id=1, source_target_pairs={{0,8},{4,12},{8,0},{12,4},{16,24},{20,28},{24,16},{28,20},{1,9},{5... | collective-permute-start | bytes 393224 | tf_op jit(solution)/shard_map/ppermute | solution.py:8
  59.2 4.9 %collective-permute-start.2 = (f32[1,2,64,128]{3,2,0,1:T(8,128)S(1)}, f32[1,2,64,128]{3,2,0,1:T(8,128)S(1)}, u32[]{:S(2)}, u32[]{:S(2)}) collective-permute-start(f32[1,2,64,128]{3,2,0,1:T(8,128)S(1)} %slice_add_fusion.1), channel_id=1, source_target_pairs={{0,16},{4,20},{8,24},{12,28},{16,0},{20,4},{24,8},{28,12},{1,17},{... | collective-permute-start | bytes 196616 | tf_op jit(solution)/shard_map/ppermute | solution.py:8
Sparse Core Ops, SparseCore 0:
  13.0 38.0 all-reduce.1
where the time goes:
time: 75.5 us; the launch traced here: 75.2 us
  blocking collectives  29.7 us (39%)
  matrix products  20.8 us (28%)
  between operations  14.3 us (19%)
  other arithmetic  4.35 us (6%)
  starting transfers between devices  2.77 us (4%)
  local copies, waits for them, and re-layouts  1.91 us (3%)
  waiting for transfers between devices  1.38 us (2%)
    all_gather x1, blocking collectives, on_device(): leaf_points = lax.all_gather(scaled, 'cols', axis=1, tiled=True)  15 us
    all_gather x1, blocking collectives, on_device(): leaf_signs = lax.all_gather(signs_half, 'cols', axis=1, tiled=True)  14.7 us
    dot_general x4, matrix products, on_device(): jnp.dot(block_signs, slope_half, preferred_element_type=jnp.float32)  4.86 us
    dot_general x4, matrix products, on_device(): jnp.dot(block_signs, kernel_half, preferred_element_type=jnp.float32)  4.57 us
    dot_general x3, matrix products, on_device(): jnp.dot(first, dfactor_stack[level].T, precision=highest)  3.17 us
    dot_general x3, matrix products, on_device(): jnp.dot(second, factor_stack[level].T, precision=highest)  2.95 us
    dot_general x3, matrix products, on_device(): value = jnp.dot(first, factor_stack[level].T, precision=highest)  2.95 us
    ppermute x3, starting transfers between devices, swapped(): lax.ppermute(array, axis, [(i, i ^ 1 << apart) for i in range(lax.axis_si...  2.77 us
  transfers between devices with their start and end apart: 4, of which 2 were waited for; matrix products, arithmetic and copies ran while one was open for 22% of the time, Pallas kernels for 0%

commit v1 on v0

--- a/solution.py
+++ b/solution.py
@@ -2,6 +2,14 @@
 import jax.numpy as jnp
 from jax import lax
 from jax.sharding import PartitionSpec as P
+
+
+def fit_rates(xin, v0, mesh_ax):
+    return jnp.split(
+        jax.lax.all_gather(jnp.concatenate([xin, v0], 0), mesh_ax, tiled=True, axis=1),
+        [xin.shape[0]],
+        0,
+    )
 
 
 def swapped(array, axis, apart):
@@ -26,8 +34,7 @@
     groups = lax.axis_size("cols")
     rows_index = lax.axis_index("rows")
     levels = lax.axis_size("rows").bit_length() - 1
-    leaf_points = lax.all_gather(scaled, "cols", axis=1, tiled=True)
-    leaf_signs = lax.all_gather(signs_half, "cols", axis=1, tiled=True)
+    leaf_points, leaf_signs = fit_rates(scaled, signs_half, "cols")
     accumulated = jnp.zeros((2, probes.shape[0], width), jnp.float32)
     for row_block in range(groups):
         block_points = leaf_points[:, row_block * width : (row_block + 1) * width]

time: 75.5 us -> 75.7 us (level)
  blocking collectives: 29.7 us -> 21.7 us
  waiting for transfers between devices: 1.38 us -> 9.34 us
    psum x1, waiting for transfers between devices: 0.02 us -> 8.15 us  [on_device(): lax.psum(jnp.stack([own_project, own_dproject], axis=1), 'cols')]
    all_gather x2 -> x1, blocking collectives: 29.7 us -> 21.7 us  [fit_rates(): jax.lax.all_gather(jnp.concatenate([xin, v0], 0), mesh_ax, tiled=True, ax...]
  transfers between devices with their start and end apart: 4 -> 4, of which waited for: 2 -> 3; matrix products, arithmetic and copies ran while one was open for 22% -> 22% of each run, Pallas kernels for 0% -> 0%
where the time goes in v1:
time: 75.7 us; the launch traced here: 75.4 us
  blocking collectives  21.7 us (29%)
  matrix products  20.8 us (27%)
  between operations  14.3 us (19%)
  waiting for transfers between devices  9.34 us (12%)
  other arithmetic  4.37 us (6%)
  starting transfers between devices  2.99 us (4%)
  local copies, waits for them, and re-layouts  1.93 us (3%)
    all_gather x1, blocking collectives, fit_rates(): jax.lax.all_gather(jnp.concatenate([xin, v0], 0), mesh_ax, tiled=True, ax...  21.7 us
    psum x1, waiting for transfers between devices, on_device(): lax.psum(jnp.stack([own_project, own_dproject], axis=1), 'cols')  8.15 us
    dot_general x4, matrix products, on_device(): jnp.dot(block_signs, slope_half, preferred_element_type=jnp.float32)  4.86 us
    dot_general x4, matrix products, on_device(): jnp.dot(block_signs, kernel_half, preferred_element_type=jnp.float32)  4.57 us
    dot_general x3, matrix products, on_device(): jnp.dot(first, dfactor_stack[level].T, precision=highest)  3.17 us
    ppermute x3, starting transfers between devices, swapped(): lax.ppermute(array, axis, [(i, i ^ 1 << apart) for i in range(lax.axis_si...  2.99 us
    dot_general x3, matrix products, on_device(): jnp.dot(second, factor_stack[level].T, precision=highest)  2.95 us
    dot_general x3, matrix products, on_device(): value = jnp.dot(first, factor_stack[level].T, precision=highest)  2.95 us
  transfers between devices with their start and end apart: 4, of which 3 were waited for; matrix products, arithmetic and copies ran while one was open for 22% of the time, Pallas kernels for 0%

profile of v1, /device:TPU:0, one launch (start us, length us, event | category | flops | bytes accessed | tf_op | source)
XLA Modules:
  0.0 75.4 jit_solution(4288899651698319164)
XLA Ops:
  6.5 0.0 all-reduce.2.cloned.1.call-start
  6.5 0.7 copy-done.4
  7.2 0.0 copy-done.3
  7.3 0.1 convert_multiply_fusion
  8.0 0.8 %bitcast_multiply_fusion.2 = (f32[8,128]{1,0:T(8,128)S(1)}, f32[8,128]{1,0:T(8,128)S(1)}, f32[8,128]{1,0:T(8,128)S(1)}) fusion(f32[14,8,128]{2,1,0:T(8,128)} %param.14, s32[]{:T(128)S(6)} %select_n.30, f32[8]{0:T(128)S(1)} %get-tuple-element.30, s32[]{:T(128)S(6)} %select_n.32, s32[]{:T(128)S(6)} %select_n.31), kind=kLoop, calls=%fused_computation.139 | loop fusion | flops 3072 | bytes 24620 | tf_op jit(solution)/shard_map/mul | solution.py:59
  8.8 0.6 exponential_multiply_fusion.17
  9.4 0.6 exponential_multiply_fusion.16
  10.1 0.0 copy-start.1
  10.1 0.6 exponential_multiply_fusion.18
  10.7 0.3 copy-done.1
  11.0 0.6 convolution_bitcast_fusion.12
  11.6 0.6 convolution_bitcast_fusion.11
  12.1 0.7 pad_maximum_fusion
  12.8 0.0 all-reduce.2.cloned.1.call-update
  12.9 21.7 %all_gather.3 = f32[72,2048]{1,0:T(8,128)S(1)} all-gather(f32[72,512]{1,0:T(8,128)S(1)} %pad_maximum_fusion.1), channel_id=1, replica_groups=mesh['rows'=8,'cols'=4] {'cols'}, dimensions={1}, use_global_device_ids=true | all-gather | bytes 737280 | tf_op jit(solution)/shard_map/all_gather | solution.py:9
  34.6 0.8 %copy-done = f32[128,128]{1,0:T(8,128)S(1)} copy-done((f32[128,128]{1,0:T(8,128)S(1)}, f32[128,128]{1,0:T(8,128)}, u32[]{:S(2)}) %copy-start) | copy-done | bytes 65560
  35.4 0.1 copy.7
  35.5 1.1 %convolution_bitcast_fusion.1 = f32[1,64,512]{2,1,0:T(8,128)S(1)} fusion(f32[]{:T(128)} %bitcast.180, f32[512]{0:T(512)S(1)} %bitcast.377, f32[512]{0:T(512)S(1)} %bitcast.379, f32[512]{0:T(512)S(1)} %bitcast.381, f32[512]{0:T(512)S(1)} %bitcast.383, f32[512]{0:T(512)S(1)} %bitcast.385, f32[512]{0:T(512)S(1)} %bitcast.387, f32[512]{0:T(512)S(1)} %bitcast.389, ...), kind=kOutput, calls=%fused_computation.1 | convolution fusion | flops 40370176 | bytes 229380 | tf_op jit(solution)/shard_map/dot_general | solution.py:48
  36.7 1.2 %convolution_bitcast_fusion = f32[1,64,512]{2,1,0:T(8,128)S(1)} fusion(f32[]{:T(128)} %bitcast.179, f32[512]{0:T(512)S(1)} %bitcast.378, f32[512]{0:T(512)S(1)} %bitcast.380, f32[512]{0:T(512)S(1)} %bitcast.382, f32[512]{0:T(512)S(1)} %bitcast.384, f32[512]{0:T(512)S(1)} %bitcast.386, f32[512]{0:T(512)S(1)} %bitcast.388, f32[512]{0:T(512)S(1)} %bitcast.390, ...), kind=kOutput, calls=%fused_computation | convolution fusion | flops 40632320 | bytes 229380 | tf_op jit(solution)/shard_map/dot_general | solution.py:49
  37.9 1.1 %convolution_bitcast_fusion.3 = f32[1,64,512]{2,1,0:T(8,128)S(1)} fusion(f32[]{:T(128)} %bitcast.181, f32[512]{0:T(512)S(1)} %bitcast.359, f32[512]{0:T(512)S(1)} %bitcast.361, f32[512]{0:T(512)S(1)} %bitcast.363, f32[512]{0:T(512)S(1)} %bitcast.365, f32[512]{0:T(512)S(1)} %bitcast.367, f32[512]{0:T(512)S(1)} %bitcast.369, f32[512]{0:T(512)S(1)} %bitcast.371, ...), kind=kOutput, calls=%fused_computation.3 | convolution fusion | flops 40370176 | bytes 229380 | tf_op jit(solution)/shard_map/dot_general | solution.py:48
  39.1 1.2 %convolution_bitcast_fusion.2 = f32[1,64,512]{2,1,0:T(8,128)S(1)} fusion(f32[]{:T(128)} %bitcast.178, f32[512]{0:T(512)S(1)} %bitcast.360, f32[512]{0:T(512)S(1)} %bitcast.362, f32[512]{0:T(512)S(1)} %bitcast.364, f32[512]{0:T(512)S(1)} %bitcast.366, f32[512]{0:T(512)S(1)} %bitcast.368, f32[512]{0:T(512)S(1)} %bitcast.370, f32[512]{0:T(512)S(1)} %bitcast.372, ...), kind=kOutput, calls=%fused_computation.2 | convolution fusion | flops 40632320 | bytes 229380 | tf_op jit(solution)/shard_map/dot_general | solution.py:49
  40.3 1.1 %convolution_bitcast_fusion.5 = f32[1,64,512]{2,1,0:T(8,128)S(1)} fusion(f32[]{:T(128)} %bitcast.182, f32[512]{0:T(512)S(1)} %bitcast.353, f32[512]{0:T(512)S(1)} %bitcast.355, f32[512]{0:T(512)S(1)} %bitcast.357, f32[512]{0:T(512)S(1)} %bitcast.409, f32[512]{0:T(512)S(1)} %bitcast.411, f32[512]{0:T(512)S(1)} %bitcast.413, f32[512]{0:T(512)S(1)} %bitcast.415, ...), kind=kOutput, calls=%fused_computation.5 | convolution fusion | flops 40370176 | bytes 229380 | tf_op jit(solution)/shard_map/dot_general | solution.py:48
  41.4 1.2 %convolution_bitcast_fusion.4 = f32[1,64,512]{2,1,0:T(8,128)S(1)} fusion(f32[]{:T(128)} %bitcast.177, f32[512]{0:T(512)S(1)} %bitcast.354, f32[512]{0:T(512)S(1)} %bitcast.356, f32[512]{0:T(512)S(1)} %bitcast.358, f32[512]{0:T(512)S(1)} %bitcast.410, f32[512]{0:T(512)S(1)} %bitcast.412, f32[512]{0:T(512)S(1)} %bitcast.414, f32[512]{0:T(512)S(1)} %bitcast.416, ...), kind=kOutput, calls=%fused_computation.4 | convolution fusion | flops 40632320 | bytes 229380 | tf_op jit(solution)/shard_map/dot_general | solution.py:49
  42.7 1.1 %convolution_bitcast_fusion.7 = f32[1,64,512]{2,1,0:T(8,128)S(1)} fusion(f32[]{:T(128)} %bitcast.173, f32[512]{0:T(512)S(1)} %bitcast.222, f32[512]{0:T(512)S(1)} %bitcast.391, f32[512]{0:T(512)S(1)} %bitcast.242, f32[512]{0:T(512)S(1)} %bitcast.393, f32[512]{0:T(512)S(1)} %bitcast.262, f32[512]{0:T(512)S(1)} %bitcast.395, f32[512]{0:T(512)S(1)} %bitcast.282, ...), kind=kOutput, calls=%fused_computation.7 | convolution fusion | flops 40370176 | bytes 229380 | tf_op jit(solution)/shard_map/dot_general | solution.py:48
  43.8 8.1 %all-reduce.2.cloned.1.call-done = f32[3,2,64,128]{3,2,0,1:T(8,128)} async-done(((f32[3,2,64,128]{3,2,0,1:T(8,128)}), f32[3,2,64,128]{3,2,0,1:T(8,128)}) %all-reduce.2.cloned.1.call-update) | async-done | bytes 196624 | tf_op jit(solution)/shard_map/psum | solution.py:67
  52.0 0.0 collective-permute-start
  52.0 1.2 %convolution_bitcast_fusion.6 = f32[1,64,512]{2,1,0:T(8,128)S(1)} fusion(f32[]{:T(128)} %bitcast.176, f32[512]{0:T(512)S(1)} %bitcast.223, f32[512]{0:T(512)S(1)} %bitcast.392, f32[512]{0:T(512)S(1)} %bitcast.243, f32[512]{0:T(512)S(1)} %bitcast.394, f32[512]{0:T(512)S(1)} %bitcast.263, f32[512]{0:T(512)S(1)} %bitcast.396, f32[512]{0:T(512)S(1)} %bitcast.283, ...), kind=kOutput, calls=%fused_computation.6 | convolution fusion | flops 40632320 | bytes 229380 | tf_op jit(solution)/shard_map/dot_general | solution.py:49
  53.2 0.4 collective-permute-done
  53.6 1.5 %collective-permute-start.1 = (f32[2,2,64,128]{3,2,0,1:T(8,128)S(1)}, f32[2,2,64,128]{3,2,0,1:T(8,128)S(1)}, u32[]{:S(2)}, u32[]{:S(2)}) collective-permute-start(f32[2,2,64,128]{3,2,0,1:T(8,128)S(1)} %slice_add_fusion), channel_id=1, source_target_pairs={{0,8},{4,12},{8,0},{12,4},{16,24},{20,28},{24,16},{28,20},{1,9},{5... | collective-permute-start | bytes 393224 | tf_op jit(solution)/shard_map/ppermute | solution.py:16
  55.1 0.2 fusion.84
  55.3 1.0 %fusion.46 = f32[64,512]{1,0:T(8,128)S(1)} fusion(f32[64,128]{1,0:T(8,128)S(1)} %fusion.84, f32[]{:T(128)} %bitcast.183, f32[128]{0:T(128)S(1)} %get-tuple-element.81, f32[512]{0:T(512)S(1)} %bitcast.224, f32[128]{0:T(128)S(1)} %get-tuple-element.82, f32[512]{0:T(512)S(1)} %bitcast.244, f32[128]{0:T(128)S(1)} %get-tuple-element.83, f32[512]{0:T(512)S(1)} %bitcast.264, ...), kind=kOutput, calls=%fused_computation.75 | convolution fusion | flops 52035584 | bytes 184324 | tf_op jit(solution)/shard_map/dot_general | solution.py:81
  56.3 0.2 fusion.83
  56.5 1.0 %fusion.2 = f32[1,64,512]{2,1,0:T(8,128)S(1)} fusion(f32[64,512]{1,0:T(8,128)S(1)} %fusion.46, f32[64,128]{1,0:T(8,128)S(1)} %fusion.83, f32[]{:T(128)} %bitcast.184, f32[128]{0:T(128)S(1)} %get-tuple-element.81, f32[512]{0:T(512)S(1)} %bitcast.225, f32[128]{0:T(128)S(1)} %get-tuple-element.82, f32[512]{0:T(512)S(1)} %bitcast.245, ...), kind=kOutput, calls=%fused_computation.16 | convolution fusion | flops 52002816 | bytes 315396 | tf_op jit(solution)/shard_map/dot_general | solution.py:81
  57.5 1.0 %convolution_bitcast_fusion.10 = f32[1,64,512]{2,1,0:T(8,128)S(1)} fusion(f32[64,128]{1,0:T(8,128)S(1)} %fusion.84, f32[]{:T(128)} %bitcast.175, f32[128]{0:T(128)S(1)} %get-tuple-element.81, f32[512]{0:T(512)S(1)} %bitcast.226, f32[128]{0:T(128)S(1)} %get-tuple-element.82, f32[512]{0:T(512)S(1)} %bitcast.246, f32[128]{0:T(128)S(1)} %get-tuple-element.83, ...), kind=kOutput, calls=%fused_computation.10 | convolution fusion | flops 51970048 | bytes 184324 | tf_op jit(solution)/shard_map/dot_general | solution.py:80
  58.5 0.7 collective-permute-done.1
  59.2 1.5 %collective-permute-start.2 = (f32[1,2,64,128]{3,2,0,1:T(8,128)S(1)}, f32[1,2,64,128]{3,2,0,1:T(8,128)S(1)}, u32[]{:S(2)}, u32[]{:S(2)}) collective-permute-start(f32[1,2,64,128]{3,2,0,1:T(8,128)S(1)} %slice_add_fusion.1), channel_id=1, source_target_pairs={{0,16},{4,20},{8,24},{12,28},{16,0},{20,4},{24,8},{28,12},{1,17},{... | collective-permute-start | bytes 196616 | tf_op jit(solution)/shard_map/ppermute | solution.py:16
  60.7 0.2 fusion.82
  60.9 1.2 %fusion.44 = f32[64,512]{1,0:T(8,128)S(1)} fusion(f32[64,128]{1,0:T(8,128)S(1)} %fusion.82, f32[]{:T(128)} %bitcast.185, f32[128]{0:T(128)S(1)} %get-tuple-element.110, f32[128]{0:T(128)S(1)} %get-tuple-element.109, f32[128]{0:T(128)S(1)} %get-tuple-element.108, f32[128]{0:T(128)S(1)} %get-tuple-element.107, f32[128]{0:T(128)S(1)} %get-tuple-element.106, ...), kind=kOutput, calls=%fused_computation.71 | convolution fusion | flops 52035584 | bytes 184324 | tf_op jit(solution)/shard_map/dot_general | solution.py:81
  62.1 0.2 fusion.81
  62.3 1.0 %fusion.1 = f32[1,64,512]{2,1,0:T(8,128)S(1)} fusion(f32[64,512]{1,0:T(8,128)S(1)} %fusion.44, f32[64,128]{1,0:T(8,128)S(1)} %fusion.81, f32[]{:T(128)} %bitcast.186, f32[128]{0:T(128)S(1)} %get-tuple-element.110, f32[128]{0:T(128)S(1)} %get-tuple-element.109, f32[128]{0:T(128)S(1)} %get-tuple-element.108, f32[128]{0:T(128)S(1)} %get-tuple-element.107, ...), kind=kOutput, calls=%fused_computation.14 | convolution fusion | flops 52002816 | bytes 315396 | tf_op jit(solution)/shard_map/dot_general | solution.py:81
  63.3 1.0 %convolution_bitcast_fusion.9 = f32[1,64,512]{2,1,0:T(8,128)S(1)} fusion(f32[64,128]{1,0:T(8,128)S(1)} %fusion.82, f32[]{:T(128)} %bitcast.190, f32[128]{0:T(128)S(1)} %get-tuple-element.110, f32[128]{0:T(128)S(1)} %get-tuple-element.109, f32[128]{0:T(128)S(1)} %get-tuple-element.108, f32[128]{0:T(128)S(1)} %get-tuple-element.107, ...), kind=kOutput, calls=%fused_computation.9 | convolution fusion | flops 51970048 | bytes 184324 | tf_op jit(solution)/shard_map/dot_general | solution.py:80
  64.3 0.0 collective-permute-done.2
  64.3 0.2 fusion.80
  64.5 1.0 %convolution_bitcast_fusion.8 = f32[1,64,512]{2,1,0:T(8,128)S(1)} fusion(f32[64,128]{1,0:T(8,128)S(1)} %fusion.80, f32[]{:T(128)} %bitcast.189, f32[128]{0:T(128)S(1)} %get-tuple-element.97, f32[128]{0:T(128)S(1)} %get-tuple-element.98, f32[128]{0:T(128)S(1)} %get-tuple-element.99, f32[128]{0:T(128)S(1)} %get-tuple-element.100, ...), kind=kOutput, calls=%fused_computation.8 | convolution fusion | flops 51970048 | bytes 184324 | tf_op jit(solution)/shard_map/dot_general | solution.py:80
  65.5 1.0 %fusion.42 = f32[64,512]{1,0:T(8,128)S(1)} fusion(f32[64,128]{1,0:T(8,128)S(1)} %fusion.80, f32[]{:T(128)} %bitcast.187, f32[128]{0:T(128)S(1)} %get-tuple-element.97, f32[128]{0:T(128)S(1)} %get-tuple-element.98, f32[128]{0:T(128)S(1)} %get-tuple-element.99, f32[128]{0:T(128)S(1)} %get-tuple-element.100, f32[128]{0:T(128)S(1)} %get-tuple-element.101, ...), kind=kOutput, calls=%fused_computation.67 | convolution fusion | flops 52035584 | bytes 184324 | tf_op jit(solution)/shard_map/dot_general | solution.py:81
  66.4 0.2 fusion.79
  66.6 1.0 %fusion = f32[1,64,512]{2,1,0:T(8,128)S(1)} fusion(f32[64,512]{1,0:T(8,128)S(1)} %fusion.42, f32[64,128]{1,0:T(8,128)S(1)} %fusion.79, f32[]{:T(128)} %bitcast.188, f32[128]{0:T(128)S(1)} %get-tuple-element.97, f32[128]{0:T(128)S(1)} %get-tuple-element.98, f32[128]{0:T(128)S(1)} %get-tuple-element.99, f32[128]{0:T(128)S(1)} %get-tuple-element.100, ...), kind=kOutput, calls=%fused_computation.12 | convolution fusion | flops 52002816 | bytes 315396 | tf_op jit(solution)/shard_map/dot_general | solution.py:81
  67.6 0.9 %fusion.41 = f32[2,64,512]{2,1,0:T(8,128)} fusion(f32[1,64,512]{2,1,0:T(8,128)S(1)} %convolution_bitcast_fusion.6, f32[1,64,512]{2,1,0:T(8,128)S(1)} %convolution_bitcast_fusion.7, f32[1,64,512]{2,1,0:T(8,128)S(1)} %convolution_bitcast_fusion.4, f32[1,64,512]{2,1,0:T(8,128)S(1)} %convolution_bitcast_fusion.5, ...), kind=kLoop, calls=%fused_computation.66 | loop fusion | flops 851968 | bytes 2097152 | tf_op jit(solution)/shard_map/add | solution.py:84
  (15 shorter events, 0.1 us)
Async XLA Ops:
  6.5 0.7 copy-start.3
  6.5 45.4 %all-reduce.2.cloned.1.call-start = ((), (), s32[]{:S(2)}) async-start(), calls=%async_computation | async-start | bytes 393216 | tf_op jit(solution)/shard_map/psum | solution.py:67
  6.5 0.7 copy-start.4
  10.1 0.9 %copy-start.1 = (f32[64,512]{1,0:T(8,128)S(1)}, f32[64,512]{1,0:T(8,128)}, u32[]{:S(2)}) copy-start(f32[64,512]{1,0:T(8,128)} %param.11) | copy-start | bytes 393220
  34.6 0.8 %copy-start = (f32[128,128]{1,0:T(8,128)S(1)}, f32[128,128]{1,0:T(8,128)}, u32[]{:S(2)}) copy-start(f32[128,128]{1,0:T(8,128)} %param.15) | copy-start | bytes 196612
  52.0 1.7 %collective-permute-start = (f32[3,2,64,128]{3,2,0,1:T(8,128)}, f32[3,2,64,128]{3,2,0,1:T(8,128)S(1)}, u32[]{:S(2)}, u32[]{:S(2)}) collective-permute-start(f32[3,2,64,128]{3,2,0,1:T(8,128)} %all-reduce.2.cloned.1.call-done), channel_id=1, source_target_pairs={{0,4},{4,0},{8,12},{12,8},{16,20},{20,16},{24,28},{28,24},{1,5},{5... | collective-permute-start | bytes 589832 | tf_op jit(solution)/shard_map/ppermute | solution.py:16
  52.0 1.7 %copy-start.2 = (f32[3,2,64,128]{3,2,0,1:T(8,128)S(1)}, f32[3,2,64,128]{3,2,0,1:T(8,128)}, u32[]{:S(2)}) copy-start(f32[3,2,64,128]{3,2,0,1:T(8,128)} %all-reduce.2.cloned.1.call-done) | copy-start | bytes 589828
  53.6 5.6 %collective-permute-start.1 = (f32[2,2,64,128]{3,2,0,1:T(8,128)S(1)}, f32[2,2,64,128]{3,2,0,1:T(8,128)S(1)}, u32[]{:S(2)}, u32[]{:S(2)}) collective-permute-start(f32[2,2,64,128]{3,2,0,1:T(8,128)S(1)} %slice_add_fusion), channel_id=1, source_target_pairs={{0,8},{4,12},{8,0},{12,4},{16,24},{20,28},{24,16},{28,20},{1,9},{5... | collective-permute-start | bytes 393224 | tf_op jit(solution)/shard_map/ppermute | solution.py:16
  59.2 5.0 %collective-permute-start.2 = (f32[1,2,64,128]{3,2,0,1:T(8,128)S(1)}, f32[1,2,64,128]{3,2,0,1:T(8,128)S(1)}, u32[]{:S(2)}, u32[]{:S(2)}) collective-permute-start(f32[1,2,64,128]{3,2,0,1:T(8,128)S(1)} %slice_add_fusion.1), channel_id=1, source_target_pairs={{0,16},{4,20},{8,24},{12,28},{16,0},{20,4},{24,8},{28,12},{1,17},{... | collective-permute-start | bytes 196616 | tf_op jit(solution)/shard_map/ppermute | solution.py:16
Sparse Core Ops, SparseCore 0:
  13.0 38.9 all-reduce.1
